TPU v7x, 512 devices: a whole 4x8x8 slice. The times are simulated.
512 devices in a mesh: dp: 8 (over z), frame: 32 (over y_hi, x, core), tile: 2 (over y_lo).
Axes of the slice: x: 4, y: 8 (y_hi: 4, y_lo: 2; y = y_hi * 2 + y_lo), z: 8, core: 2. Of those that a mesh axis runs over, the one named last changes fastest.
Arguments:
- clip_input: bfloat16 [8, 32, 18, 32, 640], P('dp', 'frame', 'tile'), may hold values from -36 to 36
- cotangent: bfloat16 [8, 32, 18, 32, 640], P('dp', 'frame', 'tile'), may hold values from -6 to 6
- norm_gain: float32 [640], replicated, may hold values from 0.25 to 1.75
- conv_weight: bfloat16 [9, 640, 640], P(None, ('frame', 'tile')), may hold values from -0.078125 to 0.078125
- attn_weight: bfloat16 [640, 2560], P(('frame', 'tile')), may hold values from -0.25 to 0.25
- query_gain: float32 [64], replicated, may hold values from 0.5 to 1.5
- key_gain: float32 [64], replicated, may hold values from 0.5 to 1.5
- logit_scale: float32 [10], replicated, may hold values from 0.5 to 4
Outputs:
- mid_grad: bfloat16 [8, 32, 18, 32, 640], P('dp', 'frame', 'tile')
- value_grad: float32 [640, 640], P(('frame', 'tile'))
- out_proj_grad: float32 [640, 640], P(('frame', 'tile'))
- query_gain_grad: float32 [64], replicated
- key_gain_grad: float32 [64], replicated
- scale_grad: float32 [10], replicated
All inputs are finite; a program needn't handle non-finite values.
Results may differ from a plain program's by a relative error of at most 0.013.
The roundings to bfloat16 on the way count: a program that leaves them out, or rounds other values in their place, can miss the bound.
Values may be sent and summed in bfloat16 or wider, within the bound.
A program may use at most 128 MiB of HBM per device.

v0:
```python
import math

import jax
import jax.numpy as jnp
from jax import lax
from jax.sharding import PartitionSpec as P

GROUPS = 32


def extended(x, sides, width):
    for axis, dim in sides:
        devices, length = (lax.axis_size(axis), x.shape[dim])
        up = [(i, (i + 1) % devices) for i in range(devices - 1)]
        down = [(j, i) for i, j in up]
        last = lax.slice_in_dim(x, length - width, length, axis=dim)
        first = lax.slice_in_dim(x, 0, width, axis=dim)
        before = lax.ppermute(last, axis, up)
        after = lax.ppermute(first, axis, down)
        x = jnp.concatenate([before, x, after], axis=dim)
    return x


def layer_stats(vec):
    mean = jnp.mean(vec, axis=-1, keepdims=True)
    cent = vec - mean
    var = jnp.mean(cent * cent, axis=-1, keepdims=True)
    rstd = lax.rsqrt(var + 1e-05)
    return (cent * rstd, rstd)


def layer_back(dhat, hat, rstd):
    first = jnp.mean(dhat, axis=-1, keepdims=True)
    second = jnp.mean(dhat * hat, axis=-1, keepdims=True)
    return rstd * (dhat - first - hat * second)


def attention_pass(mid, cot, weights, query_gain, key_gain, logit_scale):
    frames, count, width = mid.shape
    heads = logit_scale.shape[0]
    depth = width // heads
    total = frames * count
    high = lax.Precision.HIGHEST
    f32 = jnp.float32
    flat = mid.reshape(total, width)
    w_inner = weights[:, : 3 * width]
    proj = jnp.dot(flat, w_inner, preferred_element_type=f32)
    query = proj[:, :width].reshape(frames, count, heads, depth)
    keyed = proj[:, width : 2 * width].reshape(frames, count, heads, depth)
    value = proj[:, 2 * width :].astype(jnp.bfloat16).reshape(frames, count, heads, depth)
    q_hat, q_rstd = layer_stats(query)
    k_hat, k_rstd = layer_stats(keyed)
    q_norm = q_hat * query_gain
    k_norm = k_hat * key_gain
    root = math.sqrt(depth)
    raw = jnp.einsum("fnhd,gnhd->nhfg", q_norm, k_norm, precision=high) / root
    scale = logit_scale[None, :, None, None]
    expo = jnp.exp(raw * scale)
    probs = expo / jnp.sum(expo, axis=-1, keepdims=True)
    probs_b = probs.astype(jnp.bfloat16)
    mixed = jnp.einsum("nhfg,gnhd->fnhd", probs_b, value, preferred_element_type=f32)
    mixed = mixed.astype(jnp.bfloat16).reshape(total, width)
    cot_flat = cot.reshape(total, width)
    w_out = weights[:, 3 * width :]
    d_mixed = lax.dot_general(cot_flat, w_out, (((1,), (1,)), ((), ())), preferred_element_type=f32)
    d_mixed = d_mixed.astype(jnp.bfloat16).reshape(frames, count, heads, depth)
    d_probs = jnp.einsum("fnhd,gnhd->nhfg", d_mixed, value, preferred_element_type=f32)
    d_value = jnp.einsum("nhfg,fnhd->gnhd", probs_b, d_mixed, preferred_element_type=f32)
    d_value = d_value.astype(jnp.bfloat16)
    d_logits = probs * (d_probs - jnp.sum(probs * d_probs, axis=-1, keepdims=True))
    scale_term = jnp.sum(d_logits * raw, axis=(0, 2, 3))
    d_raw = d_logits * scale / root
    d_qn = jnp.einsum("nhfg,gnhd->fnhd", d_raw, k_norm, precision=high)
    d_kn = jnp.einsum("nhfg,fnhd->gnhd", d_raw, q_norm, precision=high)
    qgain_term = jnp.sum(d_qn * q_hat, axis=(0, 1, 2))
    kgain_term = jnp.sum(d_kn * k_hat, axis=(0, 1, 2))
    d_query = layer_back(d_qn * query_gain, q_hat, q_rstd).astype(jnp.bfloat16)
    d_key = layer_back(d_kn * key_gain, k_hat, k_rstd).astype(jnp.bfloat16)
    d_cat = jnp.concatenate(
        [d_query.reshape(total, width), d_key.reshape(total, width), d_value.reshape(total, width)],
        axis=1,
    )
    d_mid = lax.dot_general(d_cat, w_inner, (((1,), (1,)), ((), ())), preferred_element_type=f32)
    d_mid = d_mid.astype(jnp.bfloat16).reshape(frames, count, width)
    return (d_mid, mixed, d_value.reshape(total, width), scale_term, qgain_term, kgain_term)


def local(
    clip_input, cotangent, norm_gain, conv_weight, attn_weight, query_gain, key_gain, logit_scale
):
    source = clip_input[0]
    cot = cotangent[0]
    frames_here, rows, cols, width = source.shape
    positions = rows * cols
    per_group = width // GROUPS
    cot_flat = cot.reshape(frames_here, positions, width)
    attn_full = lax.all_gather(attn_weight, ("frame", "tile"), axis=0, tiled=True)
    xf = source.astype(jnp.float32).reshape(frames_here, positions, GROUPS, per_group)
    sums, squares = lax.psum((jnp.sum(xf, axis=(1, 3)), jnp.sum(xf * xf, axis=(1, 3))), "tile")
    count = positions * lax.axis_size("tile") * per_group
    mean = sums / count
    rstd = lax.rsqrt(squares / count - mean * mean + 1e-05)
    normed = (xf - mean[:, None, :, None]) * rstd[:, None, :, None]
    zed = normed.reshape(frames_here, rows, cols, width) * norm_gain
    act = jax.nn.silu(zed).astype(jnp.bfloat16)
    padded = extended(act, (("tile", 1),), 1)
    padded = jnp.pad(padded, ((0, 0), (0, 0), (1, 1), (0, 0)))
    slabs = []
    for row_off in (-1, 0, 1):
        for col_off in (-1, 0, 1):
            slabs.append(
                padded[:, 1 + row_off : 1 + row_off + rows, 1 + col_off : 1 + col_off + cols, :]
            )
    stacked = jnp.stack(slabs, axis=3).reshape(frames_here * positions, 9, width)
    full_conv = lax.all_gather(conv_weight, ("frame", "tile"), axis=1, tiled=True)
    pre = jnp.dot(
        stacked.reshape(frames_here * positions, 9 * width),
        full_conv.reshape(9 * width, width),
        preferred_element_type=jnp.float32,
    )
    mid = (source.astype(jnp.float32) + pre.reshape(frames_here, rows, cols, width)).astype(
        jnp.bfloat16
    )
    mid_flat = mid.reshape(frames_here, positions, width)
    mid_tiled, cot_tiled = (
        lax.all_to_all(mid_flat, "frame", split_axis=1, concat_axis=0, tiled=True),
        lax.all_to_all(cot_flat, "frame", split_axis=1, concat_axis=0, tiled=True),
    )
    d_mid, mixed, d_value, scale_term, qgain_term, kgain_term = attention_pass(
        mid_tiled, cot_tiled, attn_full, query_gain, key_gain, logit_scale
    )
    d_back = lax.all_to_all(d_mid, "frame", split_axis=0, concat_axis=1, tiled=True)
    mid_grad = (
        cot.astype(jnp.float32) + d_back.reshape(frames_here, rows, cols, width).astype(jnp.float32)
    ).astype(jnp.bfloat16)
    tiled_mid = mid_tiled.reshape(-1, width)
    tiled_cot = cot_tiled.reshape(-1, width)
    contract = (((0,), (0,)), ((), ()))
    value_term = lax.dot_general(tiled_mid, d_value, contract, preferred_element_type=jnp.float32)
    out_term = lax.dot_general(mixed, tiled_cot, contract, preferred_element_type=jnp.float32)
    shares = lax.psum_scatter(
        jnp.concatenate([value_term, out_term], axis=1),
        ("frame", "tile"),
        scatter_dimension=0,
        tiled=True,
    )
    summed = lax.psum(shares.astype(jnp.bfloat16), "dp").astype(jnp.float32)
    scale_sum, qgain_sum, kgain_sum = lax.psum(
        (scale_term, qgain_term, kgain_term), ("dp", "frame", "tile")
    )
    tokens_all = lax.axis_size("dp") * mid_tiled.shape[0] * rows * lax.axis_size("tile") * cols
    factor = 1.0 / math.sqrt(tokens_all)
    value_grad = summed[:, :width] * factor
    out_proj_grad = summed[:, width:] * factor
    return (
        mid_grad[None],
        value_grad,
        out_proj_grad,
        qgain_sum * factor,
        kgain_sum * factor,
        scale_sum * factor,
    )


def solution(mesh):
    in_specs = (
        P("dp", "frame", "tile", None, None),
        P("dp", "frame", "tile", None, None),
        P(),
        P(None, ("frame", "tile"), None),
        P(("frame", "tile"), None),
        P(),
        P(),
        P(),
    )
    out_specs = (
        P("dp", "frame", "tile", None, None),
        P(("frame", "tile"), None),
        P(("frame", "tile"), None),
        P(),
        P(),
        P(),
    )
    return jax.shard_map(local, mesh=mesh, in_specs=in_specs, out_specs=out_specs, check_vma=False)
```

profile of v0, /device:TPU:1, one launch (start us, length us, event | category | flops | bytes accessed | tf_op | source)
XLA Modules:
  0.0 950.0 jit_solution(8612890330028750961)
XLA Ops:
  11.2 4.4 all-reduce.3
  17.0 3.4 collective-permute-start
  22.8 2.9 reduce.8
  26.9 11.3 %all-to-all-start.1 = ((bf16[32,2,2880]{2,1,0:T(2,128)(2,1)}), bf16[32,2,2880]{2,1,0:T(2,128)(2,1)S(1)}, u32[]{:S(2)}, u32[]{:S(2)}) async-start(bf16[32,2,2880]{2,1,0:T(2,128)(2,1)} %reshape.273), calls=%async_computation.1 | async-start | bytes 753664 | tf_op jit(solution)/shard_map/all_to_all | solution.py:127
  39.7 4.1 copy.126
  43.9 7.3 dot_general.38
  51.2 167.2 %all-gather.4.cloned.1.call-done = bf16[9,640,640]{2,0,1:T(8,128)(2,1)} async-done(((bf16[9,10,640]{2,0,1:T(8,128)(2,1)}), bf16[9,640,640]{2,0,1:T(8,128)(2,1)}) %all-gather.4.cloned.1.call-update) | async-done | bytes 7372816 | tf_op jit(solution)/shard_map/all_gather | solution.py:115
  218.4 9.3 copy.128
  227.7 6.9 fusion.26
  235.2 2.9 reduce.9
  239.2 16.7 %all-to-all-start = ((bf16[32,2,2880]{2,1,0:T(2,128)(2,1)}), bf16[32,2,2880]{2,1,0:T(2,128)(2,1)}, u32[]{:S(2)}, u32[]{:S(2)}) async-start(bf16[32,2,2880]{2,1,0:T(2,128)(2,1)} %reshape.275), calls=%async_computation | async-start | bytes 753664 | tf_op jit(solution)/shard_map/all_to_all | solution.py:126
  259.2 164.3 %all-gather.6.cloned.1.call-done = bf16[64,10,2560]{2,1,0:T(8,128)(2,1)} async-done(((bf16[1,10,2560]{2,1,0:T(8,128)(2,1)}), bf16[64,10,2560]{2,1,0:T(8,128)(2,1)}) %all-gather.6.cloned.1.call-update) | async-done | bytes 3276816 | tf_op jit(solution)/shard_map/all_gather | solution.py:97
  423.4 5.3 reshape.268
  428.7 2.9 convolution_convert_fusion.2
  431.6 2.5 reshape.256
  434.2 3.6 reshape.276
  437.7 2.2 fusion.3
  447.5 5.0 multiply_reduce_fusion.4
  453.3 3.0 fusion.18
  458.4 3.0 multiply_reduce_fusion
  461.4 4.5 fusion.5
  465.9 5.9 fusion.6
  473.2 2.7 reshape.262
  475.9 2.5 copy.141
  480.3 2.1 fusion.90
  485.0 284.3 %all-reduce.5 = bf16[640,1280]{0,1:T(8,128)(2,1)} all-reduce(f32[640,1280]{0,1:T(8,128)} %pad_maximum_fusion), channel_id=2, replica_groups=mesh['dp'=8,'frame'=32,'tile'=2] {'frame','tile'}, use_global_device_ids=true, to_apply=%region_16.17.clone | all-reduce | flops 819200 | bytes 4915200
  770.5 28.1 %psum.44 = bf16[10,1280]{0,1:T(8,128)(2,1)} all-reduce(bf16[10,1280]{0,1:T(8,128)(2,1)S(1)} %dynamic-slice_convert_fusion), channel_id=1, replica_groups=mesh['dp'=8,'frame'=32,'tile'=2] {'dp'}, use_global_device_ids=true, to_apply=%region_17.18 | all-reduce | flops 12800 | bytes 51200 | tf_op jit(solution)/shard_map/psum | solution.py:147
  806.2 2.5 reshape.258
  811.5 2.6 reshape.259
  814.1 3.1 fusion.23
  819.2 18.8 %all-to-all-start.2 = ((bf16[32,9,640]{2,1,0:T(8,128)(2,1)}), bf16[32,9,640]{2,1,0:T(8,128)(2,1)S(1)}, u32[]{:S(2)}, u32[]{:S(2)}) async-start(bf16[32,9,640]{2,1,0:T(8,128)(2,1)} %reshape.261), calls=%async_computation.2 | async-start | bytes 1310720 | tf_op jit(solution)/shard_map/all_to_all | solution.py:132
  839.6 100.9 %all-reduce.2 = (f32[64]{0:T(128)S(1)}, f32[64]{0:T(128)S(1)}, f32[10]{0:T(128)S(1)}) all-reduce(f32[64]{0:T(128)S(1)} %get-tuple-element.44, f32[64]{0:T(128)S(1)} %get-tuple-element.42, f32[10]{0:T(128)S(1)} %copy-done.18), channel_id=1, replica_groups=mesh['dp'=8,'frame'=32,'tile'=2] {'dp','frame','tile'}, use_global_device_ids=true, to_apply=%region_19.20 | all-reduce | flops 138 | bytes 1104 | tf_op jit(solution)/shard_map/psum | solution.py:148
  (118 shorter events, 48.4 us)
Async XLA Ops:
  7.2 8.9 copy-start.7
  7.2 14.5 %copy-start.12 = (bf16[1,1,9,32,640]{4,3,2,1,0:T(8,128)(2,1)S(1)}, bf16[1,1,9,32,640]{4,3,2,1,0:T(8,128)(2,1)}, u32[]{:S(2)}) copy-start(bf16[1,1,9,32,640]{4,3,2,1,0:T(8,128)(2,1)} %param.9) | copy-start | bytes 1105924
  7.2 211.2 %all-gather.4.cloned.1.call-start = ((), (), s32[]{:S(2)}) async-start(), calls=%async_computation.3 | async-start | bytes 13312000 | tf_op jit(solution)/shard_map/all_gather | solution.py:115
  9.0 414.5 %all-gather.6.cloned.1.call-start = ((), (), s32[]{:S(2)}) async-start(), calls=%async_computation.4 | async-start | bytes 5324800 | tf_op jit(solution)/shard_map/all_gather | solution.py:97
  17.0 21.2 %collective-permute-start = (bf16[1,1,32,640]{3,2,1,0:T(8,128)(2,1)S(1)}, bf16[1,1,32,640]{3,2,1,0:T(8,128)(2,1)S(1)}, u32[]{:S(2)}, u32[]{:S(2)}) collective-permute-start(bf16[1,1,32,640]{3,2,1,0:T(8,128)(2,1)S(1)} %get-tuple-element.63), channel_id=1, source_target_pairs={{0,1},{2,3},{4,5},{6,7},{8,9},{10,11},{12,13},{14,15},{16,17},{18,... | collective-permute-start | bytes 122888 | tf_op jit(solution)/shard_map/ppermute | solution.py:18
  20.4 17.8 %collective-permute-start.1 = (bf16[1,1,32,640]{3,2,1,0:T(8,128)(2,1)S(1)}, bf16[1,1,32,640]{3,2,1,0:T(8,128)(2,1)S(1)}, u32[]{:S(2)}, u32[]{:S(2)}) collective-permute-start(bf16[1,1,32,640]{3,2,1,0:T(8,128)(2,1)S(1)} %get-tuple-element.64), channel_id=1, source_target_pairs={{1,0},{3,2},{5,4},{7,6},{9,8},{11,10},{13,12},{15,14},{17,16},{19,... | collective-permute-start | bytes 122888 | tf_op jit(solution)/shard_map/ppermute | solution.py:19
  26.9 212.4 %all-to-all-start.1 = ((bf16[32,2,2880]{2,1,0:T(2,128)(2,1)}), bf16[32,2,2880]{2,1,0:T(2,128)(2,1)S(1)}, u32[]{:S(2)}, u32[]{:S(2)}) async-start(bf16[32,2,2880]{2,1,0:T(2,128)(2,1)} %reshape.273), calls=%async_computation.1 | async-start | bytes 753664 | tf_op jit(solution)/shard_map/all_to_all | solution.py:127
  38.4 0.7 copy-start.14
  235.1 22.7 %copy-start.17 = (f32[10]{0:T(128)S(1)}, f32[10]{0:T(128)}, u32[]{:S(2)}) copy-start(f32[10]{0:T(128)} %param.15) | copy-start | bytes 124
  239.2 194.9 %all-to-all-start = ((bf16[32,2,2880]{2,1,0:T(2,128)(2,1)}), bf16[32,2,2880]{2,1,0:T(2,128)(2,1)}, u32[]{:S(2)}, u32[]{:S(2)}) async-start(bf16[32,2,2880]{2,1,0:T(2,128)(2,1)} %reshape.275), calls=%async_computation | async-start | bytes 753664 | tf_op jit(solution)/shard_map/all_to_all | solution.py:126
  428.7 9.0 copy-start.2
  444.1 1.5 copy-start
  446.1 1.4 copy-start.1
  447.5 5.1 copy-start.8
  447.5 5.1 copy-start.9
  452.7 0.7 copy-start.15
  452.7 0.7 copy-start.16
  480.3 2.8 copy-start.11
  480.3 2.1 copy-start.6
  798.7 4.7 copy-start.5
  804.8 3.9 copy-start.4
  810.1 4.0 copy-start.3
  817.1 20.8 %copy-start.10 = (f32[10,1280]{0,1:T(8,128)S(1)}, f32[10,1280]{0,1:T(8,128)}, u32[]{:S(2)}) copy-start(f32[10,1280]{0,1:T(8,128)} %convert_element_type.150) | copy-start | bytes 153604
  819.2 20.4 %copy-start.18 = (f32[10]{0:T(128)S(1)}, f32[10]{0:T(128)}, u32[]{:S(2)}) copy-start(f32[10]{0:T(128)} %get-tuple-element.71) | copy-start | bytes 124
  819.2 122.8 %all-to-all-start.2 = ((bf16[32,9,640]{2,1,0:T(8,128)(2,1)}), bf16[32,9,640]{2,1,0:T(8,128)(2,1)S(1)}, u32[]{:S(2)}, u32[]{:S(2)}) async-start(bf16[32,9,640]{2,1,0:T(8,128)(2,1)} %reshape.261), calls=%async_computation.2 | async-start | bytes 1310720 | tf_op jit(solution)/shard_map/all_to_all | solution.py:132
  837.9 104.2 %copy-start.13 = (bf16[1,1,9,32,640]{4,3,2,1,0:T(8,128)(2,1)S(1)}, bf16[1,1,9,32,640]{4,3,2,1,0:T(8,128)(2,1)}, u32[]{:S(2)}) copy-start(bf16[1,1,9,32,640]{4,3,2,1,0:T(8,128)(2,1)} %param.9) | copy-start | bytes 1105924
Sparse Core Ops, SparseCore 0:
  10.7 207.6 all-gather.3
  220.5 202.8 all-gather.5
where the time goes:
time: 956 us; the launch traced here: 950 us
  blocking collectives  418 us (44%)
  waiting for transfers between devices  332 us (35%)
  local copies, waits for them, and re-layouts  69.5 us (7%)
  starting transfers between devices  51.6 us (5%)
  matrix products  33.7 us (4%)
  other arithmetic  29.8 us (3%)
  between operations  15.5 us (2%)
    unnamed x1, blocking collectives  284 us
    all_gather x1, waiting for transfers between devices, local(): lax.all_gather(conv_weight, ('frame', 'tile'), axis=1, tiled=True)  167 us
    all_gather x1, waiting for transfers between devices, local(): lax.all_gather(attn_weight, ('frame', 'tile'), axis=0, tiled=True)  164 us
    psum x1, blocking collectives, local(): lax.psum((scale_term, qgain_term, kgain_term), ('dp', 'frame', 'tile'))  101 us
    psum x1, blocking collectives, local(): summed = lax.psum(shares.astype(jnp.bfloat16), 'dp').astype(jnp.float32)  28.1 us
    unnamed x53, local copies, waits for them, and re-layouts  19.7 us
  transfers between devices with their start and end apart: 7, of which 2 were waited for; matrix products, arithmetic and copies ran while one was open for 6% of the time, Pallas kernels for 0%

commit v1 on v0

--- a/solution.py
+++ b/solution.py
@@ -3,22 +3,111 @@
 import jax
 import jax.numpy as jnp
 from jax import lax
+from jax.experimental import pallas as pl
+from jax.experimental.pallas import tpu as pltpu
 from jax.sharding import PartitionSpec as P
 
 GROUPS = 32
 
 
-def extended(x, sides, width):
-    for axis, dim in sides:
-        devices, length = (lax.axis_size(axis), x.shape[dim])
-        up = [(i, (i + 1) % devices) for i in range(devices - 1)]
-        down = [(j, i) for i, j in up]
-        last = lax.slice_in_dim(x, length - width, length, axis=dim)
-        first = lax.slice_in_dim(x, 0, width, axis=dim)
-        before = lax.ppermute(last, axis, up)
-        after = lax.ppermute(first, axis, down)
-        x = jnp.concatenate([before, x, after], axis=dim)
-    return x
+def gather_kernel(w_ref, out_ref, send_sem, recv_sem, own_sem):
+    frame, yl = (lax.axis_index("frame"), lax.axis_index("tile"))
+    core = frame % 2
+    x = (frame // 2) % 4
+    y = (frame // 8) * 2 + yl
+
+    def place(dy, dx, dc):
+        yy, xx, cc = ((y + dy + 8) % 8, (x + dx + 4) % 4, (core + dc) % 2)
+        return ((yy // 2) * 8 + xx * 2 + cc, yy % 2)
+
+    def slot(dy, dx, dc):
+        ff, tt = place(dy, dx, dc)
+        return ff * 2 + tt
+
+    sent = []
+
+    def send(block, to, own=False):
+        ff, tt = place(*to)
+        at = slot(*block)
+        copy = pltpu.make_async_remote_copy(
+            src_ref=w_ref if own else out_ref.at[at],
+            dst_ref=out_ref.at[at],
+            send_sem=send_sem.at[len(sent)],
+            recv_sem=recv_sem.at[at],
+            device_id={"frame": ff, "tile": tt},
+            device_id_type=pl.DeviceIdType.MESH,
+        )
+        copy.start()
+        sent.append(copy)
+
+    def arrived(block):
+        at = slot(*block)
+        pltpu.make_async_remote_copy(
+            src_ref=out_ref.at[at],
+            dst_ref=out_ref.at[at],
+            send_sem=send_sem.at[0],
+            recv_sem=recv_sem.at[at],
+            device_id={"frame": frame, "tile": yl},
+            device_id_type=pl.DeviceIdType.MESH,
+        ).wait_recv()
+
+    up, down, right, left, twin = ((1, 0, 0), (-1, 0, 0), (0, 1, 0), (0, -1, 0), (0, 0, 1))
+    barrier = pltpu.get_barrier_semaphore()
+    for to in (up, down, right, left, twin):
+        ff, tt = place(*to)
+        pl.semaphore_signal(
+            barrier,
+            inc=1,
+            device_id={"frame": ff, "tile": tt},
+            device_id_type=pl.DeviceIdType.MESH,
+        )
+    pl.semaphore_wait(barrier, 5)
+    mine = pltpu.make_async_copy(w_ref, out_ref.at[slot(0, 0, 0)], own_sem)
+    mine.start()
+    for to in (right, left, up, down, twin):
+        send((0, 0, 0), to, own=True)
+    order = [0, -1, 1, -2, 2, -3, 3, -4]
+    for dy in order[1:]:
+        arrived((dy, 0, 0))
+        if dy < 0 and dy > -4:
+            send((dy, 0, 0), up)
+        if dy > 0 and dy < 3:
+            send((dy, 0, 0), down)
+        for to in (right, left, twin):
+            send((dy, 0, 0), to)
+    for k, dy in enumerate(order):
+        arrived((dy, -1, 0))
+        if k % 2 == 0:
+            send((dy, -1, 0), right)
+        send((dy, -1, 0), twin)
+        arrived((dy, 1, 0))
+        if k % 2 == 1:
+            send((dy, 1, 0), left)
+        send((dy, 1, 0), twin)
+    for dy in order:
+        arrived((dy, 2, 0))
+        send((dy, 2, 0), twin)
+    for dy in order:
+        for dx in (0, -1, 1, 2):
+            arrived((dy, dx, 1))
+    mine.wait()
+    for copy in sent:
+        copy.wait_send()
+
+
+def gathered(shard):
+    return pl.pallas_call(
+        gather_kernel,
+        out_shape=jax.ShapeDtypeStruct((64,) + shard.shape, shard.dtype),
+        in_specs=[pl.BlockSpec(memory_space=pltpu.VMEM)],
+        out_specs=pl.BlockSpec(memory_space=pl.ANY),
+        scratch_shapes=[
+            pltpu.SemaphoreType.DMA((63,)),
+            pltpu.SemaphoreType.DMA((64,)),
+            pltpu.SemaphoreType.DMA,
+        ],
+        compiler_params=pltpu.CompilerParams(collective_id=0, has_side_effects=True),
+    )(shard)
 
 
 def layer_stats(vec):
@@ -43,7 +132,7 @@
     high = lax.Precision.HIGHEST
     f32 = jnp.float32
     flat = mid.reshape(total, width)
-    w_inner = weights[:, : 3 * width]
+    w_inner = jnp.concatenate([weights[0], weights[1], weights[2]], axis=1)
     proj = jnp.dot(flat, w_inner, preferred_element_type=f32)
     query = proj[:, :width].reshape(frames, count, heads, depth)
     keyed = proj[:, width : 2 * width].reshape(frames, count, heads, depth)
@@ -61,7 +150,7 @@
     mixed = jnp.einsum("nhfg,gnhd->fnhd", probs_b, value, preferred_element_type=f32)
     mixed = mixed.astype(jnp.bfloat16).reshape(total, width)
     cot_flat = cot.reshape(total, width)
-    w_out = weights[:, 3 * width :]
+    w_out = weights[3]
     d_mixed = lax.dot_general(cot_flat, w_out, (((1,), (1,)), ((), ())), preferred_element_type=f32)
     d_mixed = d_mixed.astype(jnp.bfloat16).reshape(frames, count, heads, depth)
     d_probs = jnp.einsum("fnhd,gnhd->nhfg", d_mixed, value, preferred_element_type=f32)
@@ -85,6 +174,19 @@
     return (d_mid, mixed, d_value.reshape(total, width), scale_term, qgain_term, kgain_term)
 
 
+def exchanged(blocks, small, axes):
+    count, rows, width = blocks.shape
+    length = small.shape[0]
+    high = lax.reduce_precision(small, 8, 7)
+    row = jnp.concatenate([high, small - high]).astype(jnp.bfloat16)
+    row = jnp.pad(row, (0, width - 2 * length))
+    both = jnp.concatenate([blocks, jnp.broadcast_to(row, (count, 1, width))], axis=1)
+    got = lax.all_to_all(both, axes, split_axis=0, concat_axis=0, tiled=True)
+    total = jnp.sum(got.astype(jnp.float32), axis=0)
+    last = total[rows]
+    return (total[:rows], last[:length] + last[length : 2 * length])
+
+
 def local(
     clip_input, cotangent, norm_gain, conv_weight, attn_weight, query_gain, key_gain, logit_scale
 ):
@@ -94,16 +196,40 @@
     positions = rows * cols
     per_group = width // GROUPS
     cot_flat = cot.reshape(frames_here, positions, width)
-    attn_full = lax.all_gather(attn_weight, ("frame", "tile"), axis=0, tiled=True)
+    shard = jnp.concatenate(
+        [
+            conv_weight.reshape(90, width),
+            jnp.transpose(attn_weight.reshape(10, 4, width), (1, 0, 2)).reshape(40, width),
+        ],
+        axis=0,
+    )
+    full = gathered(shard).reshape(64, 13, 10, width).transpose(1, 0, 2, 3)
+    full = full.reshape(13, width, width)
+    full_conv, attn_full = (full[:9], full[9:])
+    tile = lax.axis_index("tile")
+    swap = [(0, 1), (1, 0)]
+    edge = jnp.where(tile == 0, source[:, rows - 1 :], source[:, :1])
+    other_edge = lax.ppermute(edge, "tile", swap)
     xf = source.astype(jnp.float32).reshape(frames_here, positions, GROUPS, per_group)
-    sums, squares = lax.psum((jnp.sum(xf, axis=(1, 3)), jnp.sum(xf * xf, axis=(1, 3))), "tile")
+    part = jnp.concatenate([jnp.sum(xf, axis=(1, 3)), jnp.sum(xf * xf, axis=(1, 3))], axis=1)
+    part = part + lax.ppermute(part, "tile", swap)
+    sums, squares = (part[:, :GROUPS], part[:, GROUPS:])
     count = positions * lax.axis_size("tile") * per_group
     mean = sums / count
     rstd = lax.rsqrt(squares / count - mean * mean + 1e-05)
-    normed = (xf - mean[:, None, :, None]) * rstd[:, None, :, None]
-    zed = normed.reshape(frames_here, rows, cols, width) * norm_gain
-    act = jax.nn.silu(zed).astype(jnp.bfloat16)
-    padded = extended(act, (("tile", 1),), 1)
+    mean_wide = jnp.repeat(mean, per_group, axis=1)[:, None, None, :]
+    rstd_wide = jnp.repeat(rstd, per_group, axis=1)[:, None, None, :]
+
+    def activated(v):
+        normed = (v.astype(jnp.float32) - mean_wide) * rstd_wide
+        return jax.nn.silu(normed * norm_gain).astype(jnp.bfloat16)
+
+    act = activated(source)
+    halo = activated(other_edge)
+    none = jnp.zeros_like(halo)
+    before = jnp.where(tile == 1, halo, none)
+    after = jnp.where(tile == 0, halo, none)
+    padded = jnp.concatenate([before, act, after], axis=1)
     padded = jnp.pad(padded, ((0, 0), (0, 0), (1, 1), (0, 0)))
     slabs = []
     for row_off in (-1, 0, 1):
@@ -112,7 +238,6 @@
                 padded[:, 1 + row_off : 1 + row_off + rows, 1 + col_off : 1 + col_off + cols, :]
             )
     stacked = jnp.stack(slabs, axis=3).reshape(frames_here * positions, 9, width)
-    full_conv = lax.all_gather(conv_weight, ("frame", "tile"), axis=1, tiled=True)
     pre = jnp.dot(
         stacked.reshape(frames_here * positions, 9 * width),
         full_conv.reshape(9 * width, width),
@@ -138,16 +263,15 @@
     contract = (((0,), (0,)), ((), ()))
     value_term = lax.dot_general(tiled_mid, d_value, contract, preferred_element_type=jnp.float32)
     out_term = lax.dot_general(mixed, tiled_cot, contract, preferred_element_type=jnp.float32)
-    shares = lax.psum_scatter(
-        jnp.concatenate([value_term, out_term], axis=1),
-        ("frame", "tile"),
-        scatter_dimension=0,
-        tiled=True,
-    )
-    summed = lax.psum(shares.astype(jnp.bfloat16), "dp").astype(jnp.float32)
-    scale_sum, qgain_sum, kgain_sum = lax.psum(
-        (scale_term, qgain_term, kgain_term), ("dp", "frame", "tile")
-    )
+    terms = jnp.concatenate([value_term, out_term], axis=1).astype(jnp.bfloat16)
+    small = jnp.concatenate([scale_term, qgain_term, kgain_term])
+    heads, depth = (logit_scale.shape[0], query_gain.shape[0])
+    plane = exchanged(terms.reshape(64, 10, 2 * width), small, ("frame", "tile"))
+    block = plane[0].astype(jnp.bfloat16)
+    summed, small = exchanged(jnp.broadcast_to(block, (8, 10, 2 * width)), plane[1], "dp")
+    scale_sum = small[:heads]
+    qgain_sum = small[heads : heads + depth]
+    kgain_sum = small[heads + depth :]
     tokens_all = lax.axis_size("dp") * mid_tiled.shape[0] * rows * lax.axis_size("tile") * cols
     factor = 1.0 / math.sqrt(tokens_all)
     value_grad = summed[:, :width] * factor

time: 956 us -> 369 us (0.39)
  the two profiles are of different devices: /device:TPU:1 before, /device:TPU:8 now
where the time goes in v1:
time: 369 us; the launch traced here: 363 us
  local copies, waits for them, and re-layouts  110 us (30%)
  waiting for transfers between devices  78.8 us (21%)
  Pallas kernels  60.9 us (17%)
  starting transfers between devices  45.3 us (12%)
  matrix products  33 us (9%)
  other arithmetic  32.9 us (9%)
    pallas_call x1, Pallas kernels, gathered(): pl.pallas_call(gather_kernel, out_shape=jax.ShapeDtypeStruct((64,) + shar...  60.9 us
    all_to_all x2, waiting for transfers between devices, exchanged(): got = lax.all_to_all(both, axes, split_axis=0, concat_axis=0, tiled=True)  56.4 us
    all_to_all x1, waiting for transfers between devices, local(): lax.all_to_all(d_mid, 'frame', split_axis=0, concat_axis=1, tiled=True)  18.2 us
    all_to_all x2, starting transfers between devices, exchanged(): got = lax.all_to_all(both, axes, split_axis=0, concat_axis=0, tiled=True)  17.2 us
    slice x2, local copies, waits for them, and re-layouts, local(): full_conv, attn_full = (full[:9], full[9:])  16.5 us
    reshape x1, local copies, waits for them, and re-layouts, local(): full_conv.reshape(9 * width, width)  14.5 us
    unnamed x58, local copies, waits for them, and re-layouts  13.8 us
    all_to_all x1, starting transfers between devices, local(): lax.all_to_all(mid_flat, 'frame', split_axis=1, concat_axis=0, tiled=True)  7.74 us
  transfers between devices with their start and end apart: 7, of which 4 were waited for; matrix products, arithmetic and copies ran while one was open for 32% of the time, Pallas kernels for 17%

profile of v1, /device:TPU:8, one launch (start us, length us, event | category | flops | bytes accessed | tf_op | source)
XLA Modules:
  0.0 362.7 jit_solution(15083442498623723607)
XLA Ops:
  2.2 7.7 %collective-permute-start.1 = (f32[1,64]{1,0:T(1,128)S(1)}, f32[1,64]{1,0:T(1,128)S(1)}, u32[]{:S(2)}, u32[]{:S(2)}) collective-permute-start(f32[1,64]{1,0:T(1,128)S(1)} %pad_maximum_fusion.6), channel_id=1, source_target_pairs={{0,1},{1,0},{2,3},{3,2},{4,5},{5,4},{6,7},{7,6},{8,9},{9,8},{10,11... | collective-permute-start | bytes 776 | tf_op jit(solution)/shard_map/ppermute | solution.py:215
  14.8 2.9 reduce.8
  18.9 5.6 %all-to-all-start.1 = ((bf16[32,2,2880]{2,1,0:T(2,128)(2,1)}), bf16[32,2,2880]{2,1,0:T(2,128)(2,1)}, u32[]{:S(2)}, u32[]{:S(2)}) async-start(bf16[32,2,2880]{2,1,0:T(2,128)(2,1)} %reshape.325), calls=%async_computation.1 | async-start | bytes 753664 | tf_op jit(solution)/shard_map/all_to_all | solution.py:252
  25.3 60.9 %shard_map.127 = bf16[64,130,640]{2,1,0:T(8,128)(2,1)} custom-call(bf16[130,640]{1,0:T(8,128)(2,1)} %pad_maximum_fusion.4.w_ref), custom_call_target="tpu_custom_call" | custom-call | tf_op jit(solution)/shard_map/pallas_call | solution.py:99
  86.2 6.7 %copy.244 = bf16[64,130,640]{2,0,1:T(8,128)(2,1)S(1)} copy(bf16[64,130,640]{2,1,0:T(8,128)(2,1)} %shard_map.127) | data formatting | bytes 21299200 | tf_op jit(solution)/shard_map/pallas_call | solution.py:99
  94.5 3.7 %slice.163 = bf16[9,64,10,640]{3,1,2,0:T(8,128)(2,1)} slice(bf16[13,64,10,640]{3,1,2,0:T(8,128)(2,1)S(1)} %bitcast.139), slice={[0:9], [0:64], [0:10], [0:640]} | slice | bytes 14745600 | tf_op jit(solution)/shard_map/slice | solution.py:208
  107.1 12.8 %copy.245 = bf16[9,64,10,640]{3,2,1,0:T(8,128)(2,1)} copy(bf16[9,64,10,640]{3,1,2,0:T(8,128)(2,1)} %slice.163) | data formatting | bytes 14745600 | tf_op jit(solution)/shard_map/slice | solution.py:208
  119.8 14.5 %reshape.319 = bf16[5760,640,1]{1,0,2:T(8,128)(2,1)} reshape(bf16[9,64,10,640]{3,2,1,0:T(8,128)(2,1)} %copy.245) | data formatting | bytes 14745600 | tf_op jit(solution)/shard_map/reshape | solution.py:243
  136.3 4.2 %copy.242 = bf16[1,9,32,9,640]{4,3,2,1,0:T(8,128)(2,1)} copy(bf16[1,9,32,9,640]{4,2,1,3,0:T(8,128)(2,1)S(1)} %fusion.66) | data formatting | bytes 6635520 | tf_op jit(solution)/shard_map/stack | solution.py:240
  140.5 7.3 %dot_general.46 = bf16[9,32,5760]{2,1,0:T(8,128)(2,1)} reshape(bf16[1,9,32,9,640]{4,3,2,1,0:T(8,128)(2,1)} %copy.242) | data formatting | bytes 6635520 | tf_op jit(solution)/shard_map/dot_general | solution.py:241
  147.8 6.9 %fusion.19 = bf16[9,32,640]{2,1,0:T(8,128)(2,1)S(1)} fusion(bf16[9,32,5760]{2,1,0:T(8,128)(2,1)} %dot_general.46, bf16[5760,640,1]{1,0,2:T(8,128)(2,1)} %reshape.319, bf16[1,1,9,32,640]{4,3,2,1,0:T(8,128)(2,1)S(1)} %copy-done.5), kind=kOutput, calls=%fused_computation.49 | convolution fusion | flops 2123919360 | bytes 11427840 | tf_op jit(solution)/shard_map/dot_general | solution.py:241
  155.3 3.7 %reduce.9 = bf16[288,640]{1,0:T(8,128)(2,1)} reduce(bf16[288,1,640]{2,1,0:T(2,128)(2,1)S(1)} %bitcast.144, bf16[]{:T(256)} %broadcast.251), dimensions={1}, to_apply=%bitcast.137.reduce_sub_computation | reduce | bytes 737282
  161.2 7.7 %all-to-all-start = ((bf16[32,2,2880]{2,1,0:T(2,128)(2,1)}), bf16[32,2,2880]{2,1,0:T(2,128)(2,1)}, u32[]{:S(2)}, u32[]{:S(2)}) async-start(bf16[32,2,2880]{2,1,0:T(2,128)(2,1)} %reshape.327), calls=%async_computation | async-start | bytes 753664 | tf_op jit(solution)/shard_map/all_to_all | solution.py:251
  171.6 3.0 reshape.326
  174.6 2.7 fusion.20
  177.3 2.5 reshape.309
  179.8 4.2 %all-to-all-done = bf16[32,2,2880]{2,1,0:T(2,128)(2,1)} async-done(((bf16[32,2,2880]{2,1,0:T(2,128)(2,1)}), bf16[32,2,2880]{2,1,0:T(2,128)(2,1)}, u32[]{:S(2)}, u32[]{:S(2)}) %all-to-all-start) | async-done | bytes 368672 | tf_op jit(solution)/shard_map/all_to_all | solution.py:251
  184.0 2.9 reshape.328
  197.5 5.0 %multiply_reduce_fusion.4 = (f32[32,9,10]{0,2,1:T(8,128)S(1)}, f32[32,9,10,64]{3,0,2,1:T(8,128)S(1)}, f32[32,9,10]{0,2,1:T(8,128)S(1)}, f32[32,9,10,64]{3,0,2,1:T(8,128)S(1)}) fusion(f32[32,9,10]{0,2,1:T(8,128)S(1)} %broadcast_multiply_fusion.4, f32[32,9,10,64]{3,2,1,0:T(8,128)} %copy-done, f32[32,9,10]{0,2,1:T(8,128)S(1)} %broadcast_multiply_fusion.5, ...), kind=kLoop, calls=%fused_computation.23 | loop fusion | flops 1100160 | bytes 2995200 | tf_op jit(solution)/shard_map/reduce_sum | solution.py:116
  203.3 3.0 fusion.14
  211.7 4.6 %fusion.1 = (f32[64]{0:T(128)S(1)}, f32[32,9,10]{0,2,1:T(8,128)}, f32[32,9,10]{0,2,1:T(8,128)}, f32[9,10,64,32]{2,3,1,0:T(8,128)}) fusion(f32[32,9,10,64]{3,0,2,1:T(8,128)S(1)} %get-tuple-element.17, f32[32,9,10]{0,2,1:T(8,128)S(1)} %add_rsqrt_fusion, f32[64]{0:T(128)S(1)} %copy-done.21, f32[9,10,32,32]{2,3,1,0:T(8,128)S(1)} %get-tuple-element.41, ...), kind=kOutput, calls=%fused_computation.7 | convolution fusion | flops 72616256 | bytes 2627368 | tf_op jit(solution)/shard_map/nhfg,fnhd->gnhd/dot_general | solution.py:163
  216.4 5.9 %fusion.2 = (f32[64]{0:T(128)S(1)}, f32[32,9,10]{0,2,1:T(8,128)}, f32[32,9,10]{0,2,1:T(8,128)}, f32[9,10,64,32]{2,3,1,0:T(8,128)}) fusion(f32[32,9,10,64]{3,0,2,1:T(8,128)S(1)} %get-tuple-element.43, f32[32,9,10]{0,2,1:T(8,128)S(1)} %add_rsqrt_fusion.1, f32[64]{0:T(128)S(1)} %copy-done.20, f32[9,10,32,32]{2,3,1,0:T(8,128)S(1)} %get-tuple-element.41, ...), kind=kOutput, calls=%fused_computation.10 | convolution fusion | flops 72616256 | bytes 2627368 | tf_op jit(solution)/shard_map/nhfg,gnhd->fnhd/dot_general | solution.py:162
  225.9 2.7 reshape.320
  239.0 2.5 copy.270
  241.5 6.9 %all-to-all-start.3 = ((bf16[64,11,1280]{2,1,0:T(8,128)(2,1)}), bf16[64,11,1280]{2,1,0:T(8,128)(2,1)}, u32[]{:S(2)}, u32[]{:S(2)}) async-start(bf16[64,11,1280]{2,1,0:T(8,128)(2,1)} %copy.270), calls=%async_computation.3 | async-start | bytes 5242880 | tf_op jit(solution)/shard_map/all_to_all | solution.py:184
  252.2 3.0 multiply_convert_fusion.1
  262.5 2.8 convolution_convert_fusion.4
  266.3 44.1 %all-to-all-done.3 = bf16[64,11,1280]{2,1,0:T(8,128)(2,1)} async-done(((bf16[64,11,1280]{2,1,0:T(8,128)(2,1)}), bf16[64,11,1280]{2,1,0:T(8,128)(2,1)}, u32[]{:S(2)}, u32[]{:S(2)}) %all-to-all-start.3) | async-done | bytes 1802272 | tf_op jit(solution)/shard_map/all_to_all | solution.py:184
  310.3 5.1 %all-to-all-start.2 = ((bf16[32,9,640]{2,1,0:T(8,128)(2,1)}), bf16[32,9,640]{2,1,0:T(8,128)(2,1)S(1)}, u32[]{:S(2)}, u32[]{:S(2)}) async-start(bf16[32,9,640]{2,1,0:T(8,128)(2,1)} %reshape.314), calls=%async_computation.2 | async-start | bytes 1310720 | tf_op jit(solution)/shard_map/all_to_all | solution.py:257
  318.7 18.2 %all-to-all-done.2 = bf16[32,9,640]{2,1,0:T(8,128)(2,1)S(1)} async-done(((bf16[32,9,640]{2,1,0:T(8,128)(2,1)}), bf16[32,9,640]{2,1,0:T(8,128)(2,1)S(1)}, u32[]{:S(2)}, u32[]{:S(2)}) %all-to-all-start.2) | async-done | bytes 368672 | tf_op jit(solution)/shard_map/all_to_all | solution.py:257
  336.9 10.3 %all-to-all-start.4 = ((bf16[8,11,1280]{2,1,0:T(8,128)(2,1)}), bf16[8,11,1280]{2,1,0:T(8,128)(2,1)S(1)}, u32[]{:S(2)}, u32[]{:S(2)}) async-start(bf16[8,11,1280]{2,1,0:T(8,128)(2,1)} %pad_maximum_fusion.3), calls=%async_computation.4 | async-start | bytes 655360 | tf_op jit(solution)/shard_map/all_to_all | solution.py:184
  348.2 12.3 %all-to-all-done.4 = bf16[8,11,1280]{2,1,0:T(8,128)(2,1)S(1)} async-done(((bf16[8,11,1280]{2,1,0:T(8,128)(2,1)}), bf16[8,11,1280]{2,1,0:T(8,128)(2,1)S(1)}, u32[]{:S(2)}, u32[]{:S(2)}) %all-to-all-start.4) | async-done | bytes 225312 | tf_op jit(solution)/shard_map/all_to_all | solution.py:184
  (156 shorter events, 74.7 us)
Async XLA Ops:
  2.2 132.1 %collective-permute-start.1 = (f32[1,64]{1,0:T(1,128)S(1)}, f32[1,64]{1,0:T(1,128)S(1)}, u32[]{:S(2)}, u32[]{:S(2)}) collective-permute-start(f32[1,64]{1,0:T(1,128)S(1)} %pad_maximum_fusion.6), channel_id=1, source_target_pairs={{0,1},{1,0},{2,3},{3,2},{4,5},{5,4},{6,7},{7,6},{8,9},{9,8},{10,11... | collective-permute-start | bytes 776 | tf_op jit(solution)/shard_map/ppermute | solution.py:215
  10.8 124.3 %collective-permute-start = (bf16[1,1,32,640]{3,2,1,0:T(8,128)(2,1)S(1)}, bf16[1,1,32,640]{3,2,1,0:T(8,128)(2,1)S(1)}, u32[]{:S(2)}, u32[]{:S(2)}) collective-permute-start(bf16[1,1,32,640]{3,2,1,0:T(8,128)(2,1)S(1)} %slice_select_fusion), channel_id=1, source_target_pairs={{0,1},{1,0},{2,3},{3,2},{4,5},{5,4},{6,7},{7,6},{8,9},{9,8},{10,11... | collective-permute-start | bytes 122888 | tf_op jit(solution)/shard_map/ppermute | solution.py:212
  14.3 10.2 %copy-start.18 = (bf16[10,2560]{1,0:T(8,128)(2,1)S(1)}, bf16[10,2560]{1,0:T(8,128)(2,1)}, u32[]{:S(2)}) copy-start(bf16[10,2560]{1,0:T(8,128)(2,1)} %param.12) | copy-start | bytes 153604
  14.8 9.8 %copy-start.17 = (bf16[9,10,640]{2,1,0:T(8,128)(2,1)S(1)}, bf16[9,10,640]{2,1,0:T(8,128)(2,1)}, u32[]{:S(2)}) copy-start(bf16[9,10,640]{2,1,0:T(8,128)(2,1)} %param.11) | copy-start | bytes 345604
  18.9 142.3 %all-to-all-start.1 = ((bf16[32,2,2880]{2,1,0:T(2,128)(2,1)}), bf16[32,2,2880]{2,1,0:T(2,128)(2,1)}, u32[]{:S(2)}, u32[]{:S(2)}) async-start(bf16[32,2,2880]{2,1,0:T(2,128)(2,1)} %reshape.325), calls=%async_computation.1 | async-start | bytes 753664 | tf_op jit(solution)/shard_map/all_to_all | solution.py:252
  119.8 15.0 %copy-start.5 = (bf16[1,1,9,32,640]{4,3,2,1,0:T(8,128)(2,1)S(1)}, bf16[1,1,9,32,640]{4,3,2,1,0:T(8,128)(2,1)}, u32[]{:S(2)}) copy-start(bf16[1,1,9,32,640]{4,3,2,1,0:T(8,128)(2,1)} %param.8) | copy-start | bytes 1105924
  119.8 15.0 %copy-start.19 = (f32[640]{0:T(1024)S(1)}, f32[640]{0:T(1024)}, u32[]{:S(2)}) copy-start(f32[640]{0:T(1024)} %param.10) | copy-start | bytes 7684
  155.3 13.7 %copy-start.3 = (bf16[640,1920]{1,0:T(8,128)(2,1)S(1)}, bf16[640,1920]{1,0:T(8,128)(2,1)}, u32[]{:S(2)}) copy-start(bf16[640,1920]{1,0:T(8,128)(2,1)} %constant_dynamic-update-slice_fusion.2) | copy-start | bytes 7372804
  161.2 22.8 %all-to-all-start = ((bf16[32,2,2880]{2,1,0:T(2,128)(2,1)}), bf16[32,2,2880]{2,1,0:T(2,128)(2,1)}, u32[]{:S(2)}, u32[]{:S(2)}) async-start(bf16[32,2,2880]{2,1,0:T(2,128)(2,1)} %reshape.327), calls=%async_computation | async-start | bytes 753664 | tf_op jit(solution)/shard_map/all_to_all | solution.py:251
  169.0 2.6 copy-start.22
  171.5 17.2 %copy-start.4 = (bf16[640,1920]{1,0:T(8,128)(2,1)}, bf16[640,1920]{1,0:T(8,128)(2,1)S(1)}, u32[]{:S(2)}) copy-start(bf16[640,1920]{1,0:T(8,128)(2,1)S(1)} %constant_dynamic-update-slice_fusion) | copy-start | bytes 7372804
  174.6 5.2 %copy-start.13 = (bf16[288,1,640]{2,1,0:T(2,128)(2,1)}, bf16[288,1,640]{2,1,0:T(2,128)(2,1)S(1)}, u32[]{:S(2)}) copy-start(bf16[288,1,640]{2,1,0:T(2,128)(2,1)S(1)} %reshape.326) | copy-start | bytes 1105924
  194.2 1.4 copy-start
  196.1 1.4 copy-start.1
  197.5 5.1 %copy-start.6 = (bf16[32,9,10,64]{3,2,1,0:T(8,128)(2,1)S(1)}, bf16[32,9,10,64]{3,2,1,0:T(8,128)(2,1)}, u32[]{:S(2)}) copy-start(bf16[32,9,10,64]{3,2,1,0:T(8,128)(2,1)} %reshape.309) | copy-start | bytes 1105924
  197.5 5.1 %copy-start.7 = (bf16[32,9,10,64]{3,2,1,0:T(8,128)(2,1)S(1)}, bf16[32,9,10,64]{3,2,1,0:T(8,128)(2,1)}, u32[]{:S(2)}) copy-start(bf16[32,9,10,64]{3,2,1,0:T(8,128)(2,1)} %reshape.310) | copy-start | bytes 1105924
  202.6 13.7 %copy-start.9 = (f32[32,9,10]{0,2,1:T(8,128)}, f32[32,9,10]{0,2,1:T(8,128)S(1)}, u32[]{:S(2)}) copy-start(f32[32,9,10]{0,2,1:T(8,128)S(1)} %add_rsqrt_fusion.1) | copy-start | bytes 34564
  202.6 0.7 copy-start.20
  202.6 0.7 copy-start.21
  216.4 5.9 %copy-start.8 = (bf16[1,288,640]{1,2,0:T(8,128)(2,1)S(1)}, bf16[1,288,640]{1,2,0:T(8,128)(2,1)}, u32[]{:S(2)}) copy-start(bf16[1,288,640]{1,2,0:T(8,128)(2,1)} %copy.277) | copy-start | bytes 1105924
  235.9 2.1 copy-start.12
  235.9 2.1 copy-start.15
  241.5 68.8 %all-to-all-start.3 = ((bf16[64,11,1280]{2,1,0:T(8,128)(2,1)}), bf16[64,11,1280]{2,1,0:T(8,128)(2,1)}, u32[]{:S(2)}, u32[]{:S(2)}) async-start(bf16[64,11,1280]{2,1,0:T(8,128)(2,1)} %copy.270), calls=%async_computation.3 | async-start | bytes 5242880 | tf_op jit(solution)/shard_map/all_to_all | solution.py:184
  248.5 3.7 %copy-start.10 = (f32[32,9,10]{0,2,1:T(8,128)S(1)}, f32[32,9,10]{0,2,1:T(8,128)}, u32[]{:S(2)}) copy-start(f32[32,9,10]{0,2,1:T(8,128)} %copy-done.9) | copy-start | bytes 34564
  255.2 4.8 %copy-start.16 = (f32[32,9,10]{0,2,1:T(8,128)S(1)}, f32[32,9,10]{0,2,1:T(8,128)}, u32[]{:S(2)}) copy-start(f32[32,9,10]{0,2,1:T(8,128)} %get-tuple-element.10) | copy-start | bytes 34564
  255.2 4.8 %copy-start.2 = (f32[9,10,64,32]{2,3,1,0:T(8,128)S(1)}, f32[9,10,64,32]{2,3,1,0:T(8,128)}, u32[]{:S(2)}) copy-start(f32[9,10,64,32]{2,3,1,0:T(8,128)} %get-tuple-element.38) | copy-start | bytes 2211844
  261.4 1.0 copy-start.14
  310.3 26.5 %all-to-all-start.2 = ((bf16[32,9,640]{2,1,0:T(8,128)(2,1)}), bf16[32,9,640]{2,1,0:T(8,128)(2,1)S(1)}, u32[]{:S(2)}, u32[]{:S(2)}) async-start(bf16[32,9,640]{2,1,0:T(8,128)(2,1)} %reshape.314), calls=%async_computation.2 | async-start | bytes 1310720 | tf_op jit(solution)/shard_map/all_to_all | solution.py:257
  317.9 29.5 %copy-start.11 = (bf16[1,1,9,32,640]{4,3,2,1,0:T(8,128)(2,1)S(1)}, bf16[1,1,9,32,640]{4,3,2,1,0:T(8,128)(2,1)}, u32[]{:S(2)}) copy-start(bf16[1,1,9,32,640]{4,3,2,1,0:T(8,128)(2,1)} %param.9) | copy-start | bytes 1105924
  336.9 23.6 %all-to-all-start.4 = ((bf16[8,11,1280]{2,1,0:T(8,128)(2,1)}), bf16[8,11,1280]{2,1,0:T(8,128)(2,1)S(1)}, u32[]{:S(2)}, u32[]{:S(2)}) async-start(bf16[8,11,1280]{2,1,0:T(8,128)(2,1)} %pad_maximum_fusion.3), calls=%async_computation.4 | async-start | bytes 655360 | tf_op jit(solution)/shard_map/all_to_all | solution.py:184
